TPU v7x, 32 devices: a whole 2x2x4 slice. The times are simulated.
32 devices in a mesh: groups: 2 (over y), ctx: 4 (over z), fsdp: 2 (over x), sub: 2 (over core).
Axes of the slice: x: 2, y: 2, z: 4, core: 2. Of those that a mesh axis runs over, the one named last changes fastest.
Arguments:
- streams: bfloat16 [3, 2048, 4096], P(None, ('groups', 'ctx', 'sub'), 'fsdp'), parts along dimension 1, may hold values from -6 to 6
- feat_taps: float32 [3, 7, 4096], P(None, None, 'fsdp'), may hold values from -2.4 to 2.4
- long_filter: bfloat16 [128, 4096], P('ctx', 'fsdp'), may hold values from -0.5 to 0.5
- upstream: bfloat16 [2048, 4096], P(('groups', 'ctx', 'sub'), 'fsdp'), parts along dimension 0, may hold values from -6 to 6
- score_dir: float32 [4096], P('fsdp'), may hold values from -21 to 21
- seg_lengths: int32 [16], P('groups'), parts along dimension 0, may hold values from 1 to 512, 1024 in all
- list_ids: int32 [16], P('groups'), parts along dimension 0, may hold values from 0 to 1
Outputs:
- d_streams: bfloat16 [3, 2048, 4096], P(None, ('groups', 'ctx', 'sub'), 'fsdp'), parts along dimension 1
- d_feat: float32 [6, 7, 4096], P('groups', None, 'fsdp'), parts along dimension 0
- d_filter: float32 [256, 4096], P(('groups', 'ctx'), 'fsdp'), parts along dimension 0
There are 2 independent parts, one for each index of `groups`. A program takes and returns all parts, laid end to end along the dimension named above; an argument that names none is the same for every part. Nothing has to cross between parts.
Inputs may be any that keep to these rules, and one draw needn't show every extreme that they name: `seg_lengths`: the lengths sum to 1024 and the longest segment has exactly 512 tokens.
All inputs are finite; a program needn't handle non-finite values.
Results may differ from a plain program's by a relative error of at most 0.012.
Values may be sent and summed in bfloat16 or wider, within the bound.
A program may use at most 64 MiB of HBM per device.

v0:
```python
import jax
import jax.numpy as jnp
from jax import lax
from jax.sharding import PartitionSpec as P

LH = 128
KF = 7
HIGH = lax.Precision.HIGHEST


def passed_along(value, axis, steps):
    count = lax.axis_size(axis)
    leading, last = (max(0, -steps), min(count, count - steps))
    return lax.ppermute(value, axis, [(source, source + steps) for source in range(leading, last)])


def tap_block(tap_count):
    return 16 if tap_count % 16 == 0 else tap_count


def segment_age(seg_lengths, positions):
    offsets = jnp.cumsum(seg_lengths, dtype=jnp.int32) - seg_lengths
    member = offsets[None, :] <= positions[:, None]
    seg_index = jnp.sum(member.astype(jnp.int32), axis=1, dtype=jnp.int32) - 1
    seg_start = jnp.max(jnp.where(member, offsets[None, :], 0), axis=1)
    return (seg_index, positions - seg_start)


def causal_taps(tap_table, extended, row_age, tok_rows):
    tap_count = tap_table.shape[0]
    per_turn = tap_block(tap_count)

    def causal_advance(b, running):
        for m in range(per_turn):
            j = b * per_turn + m
            window = lax.dynamic_slice_in_dim(extended, tap_count - 1 - j, tok_rows, 0)
            weight_row = lax.dynamic_index_in_dim(tap_table, j, 0, keepdims=False)
            running = running + jnp.where(
                (row_age >= j)[:, None], weight_row[None, :] * window.astype(jnp.float32), 0.0
            )
        return running

    start_sum = jnp.zeros((tok_rows, extended.shape[1]), jnp.float32)
    return lax.fori_loop(0, tap_count // per_turn, causal_advance, start_sum)


def reverse_taps(tap_table, extended, ext_age, tok_rows):
    tap_count = tap_table.shape[0]
    per_turn = tap_block(tap_count)

    def reverse_advance(b, running):
        for m in range(per_turn):
            j = b * per_turn + m
            window = lax.dynamic_slice_in_dim(extended, j, tok_rows, 0)
            keep = lax.dynamic_slice_in_dim(ext_age, j, tok_rows, 0) >= j
            weight_row = lax.dynamic_index_in_dim(tap_table, j, 0, keepdims=False)
            running = running + jnp.where(
                keep[:, None], weight_row[None, :] * window.astype(jnp.float32), 0.0
            )
        return running

    start_sum = jnp.zeros((tok_rows, extended.shape[1]), jnp.float32)
    return lax.fori_loop(0, tap_count // per_turn, reverse_advance, start_sum)


def correlate_taps(gradient, extended, row_age, tap_count, tok_rows):
    per_turn = tap_block(tap_count)

    def correlate_advance(b, result):
        collected = []
        for m in range(per_turn):
            j = b * per_turn + m
            window = lax.dynamic_slice_in_dim(extended, tap_count - 1 - j, tok_rows, 0)
            product = gradient.astype(jnp.float32) * window.astype(jnp.float32)
            collected.append(jnp.sum(jnp.where((row_age >= j)[:, None], product, 0.0), axis=0))
        return lax.dynamic_update_slice_in_dim(result, jnp.stack(collected), b * per_turn, 0)

    start_rows = jnp.zeros((tap_count, gradient.shape[1]), jnp.float32)
    return lax.fori_loop(0, tap_count // per_turn, correlate_advance, start_rows)


def list_coef(totals, seg_lengths, list_ids):
    length_f = seg_lengths.astype(jnp.float32)
    scores = totals / length_f
    mates = (list_ids[:, None] == list_ids[None, :]).astype(jnp.float32)
    mean_score = jnp.dot(mates, scores, precision=HIGH) / jnp.sum(mates, axis=1)
    return (scores - mean_score) / length_f


def local(streams, feat_taps, long_filter, upstream, score_dir, seg_lengths, list_ids):
    tok_rows = streams.shape[1]
    seg_count = seg_lengths.shape[0]
    first_row = lax.axis_index(("ctx", "sub")) * tok_rows
    positions = first_row + jnp.arange(tok_rows + LH - 1, dtype=jnp.int32)
    seg_span, age_span = segment_age(seg_lengths, positions)
    seg_index = seg_span[:tok_rows]
    row_age = age_span[:tok_rows]
    left_rim = passed_along(streams[:, tok_rows - (KF - 1) :, :], ("ctx", "sub"), 1)
    stream_ext = jnp.concatenate([left_rim, streams], axis=1)
    featured = [
        causal_taps(feat_taps[i], stream_ext[i], row_age, tok_rows).astype(jnp.bfloat16)
        for i in range(3)
    ]
    query, key_feat, value_feat = featured
    product = (key_feat.astype(jnp.float32) * value_feat.astype(jnp.float32)).astype(jnp.bfloat16)
    filt = lax.all_gather(long_filter, "ctx", axis=0, tiled=True).astype(jnp.float32)
    prod_rim = passed_along(product[tok_rows - (LH - 1) :], ("ctx", "sub"), 1)
    prod_ext = jnp.concatenate([prod_rim, product], axis=0)
    mixed = causal_taps(filt, prod_ext, row_age, tok_rows)
    out_y = query.astype(jnp.float32) * mixed
    projected = jnp.dot(out_y, score_dir, precision=HIGH)
    onehot = (seg_index[:, None] == jnp.arange(seg_count, dtype=jnp.int32)[None, :]).astype(
        jnp.float32
    )
    partial_sums = jnp.dot(projected, onehot, precision=HIGH)
    totals = lax.psum(partial_sums, ("ctx", "fsdp", "sub"))
    coef = list_coef(totals, seg_lengths, list_ids)
    tok_coef = jnp.dot(onehot, coef, precision=HIGH)
    d_out = upstream.astype(jnp.float32) + tok_coef[:, None] * score_dir[None, :]
    d_query = (d_out * mixed).astype(jnp.bfloat16)
    d_mixed = (d_out * query.astype(jnp.float32)).astype(jnp.bfloat16)
    grad_rim = passed_along(d_mixed[: LH - 1], ("ctx", "sub"), -1)
    dm_ext = jnp.concatenate([d_mixed, grad_rim], axis=0)
    d_prod = reverse_taps(filt, dm_ext, age_span, tok_rows)
    d_key = (d_prod * value_feat.astype(jnp.float32)).astype(jnp.bfloat16)
    d_value = (d_prod * key_feat.astype(jnp.float32)).astype(jnp.bfloat16)
    filter_part = correlate_taps(d_mixed, prod_ext, row_age, LH, tok_rows)
    grads = jnp.stack([d_query, d_key, d_value])
    feat_rim = passed_along(grads[:, : KF - 1, :], ("ctx", "sub"), -1)
    grads_ext = jnp.concatenate([grads, feat_rim], axis=1)
    d_streams = jnp.stack(
        [reverse_taps(feat_taps[i], grads_ext[i], age_span, tok_rows) for i in range(3)]
    ).astype(jnp.bfloat16)
    taps_part = jnp.stack(
        [correlate_taps(grads[i], stream_ext[i], row_age, KF, tok_rows) for i in range(3)]
    )
    shard_rows = long_filter.shape[0]
    filter_all, d_feat = lax.psum((filter_part, taps_part), ("ctx", "sub"))
    d_filter = lax.dynamic_slice_in_dim(
        filter_all, lax.axis_index("ctx") * shard_rows, shard_rows, 0
    )
    return (d_streams, d_feat, d_filter)


def solution(mesh):
    placed = (
        P(None, ("groups", "ctx", "sub"), "fsdp"),
        P(None, None, "fsdp"),
        P("ctx", "fsdp"),
        P(("groups", "ctx", "sub"), "fsdp"),
        P("fsdp"),
        P("groups"),
        P("groups"),
    )
    return jax.shard_map(
        local,
        mesh=mesh,
        in_specs=placed,
        out_specs=(
            P(None, ("groups", "ctx", "sub"), "fsdp"),
            P("groups", None, "fsdp"),
            P(("groups", "ctx"), "fsdp"),
        ),
        check_vma=False,
    )
```

profile of v0, /device:TPU:0, one launch (start us, length us, event | category | flops | bytes accessed | tf_op | source)
XLA Modules:
  0.0 389.5 jit_solution(13309928368215574927)
XLA Ops:
  8.1 2.4 collective-permute-start
  15.9 17.6 %all_gather.3 = bf16[128,2048]{1,0:T(8,128)(2,1)S(1)} all-gather(bf16[32,2048]{1,0:T(8,128)(2,1)} %param.15), channel_id=1, replica_groups=mesh['groups'=2,'ctx'=4,'fsdp'=2,'sub'=2] {'ctx'}, dimensions={0}, use_global_device_ids=true | all-gather | bytes 655360 | tf_op jit(solution)/shard_map/all_gather | solution.py:106
  33.4 9.7 %fusion.68 = (bf16[128,2048]{1,0:T(8,128)(2,1)S(1)}, bf16[128,2048]{1,0:T(8,128)(2,1)}, bf16[128,2048]{1,0:T(8,128)(2,1)}, bf16[128,2048]{1,0:T(8,128)(2,1)}) fusion(f32[2048]{0:T(1024)S(1)} %bitcast.486, pred[128]{0:T(512)(128)(4,1)S(1)} %get-tuple-element.922, f32[2048]{0:T(1024)S(1)} %bitcast.488, pred[128]{0:T(512)(128)(4,1)S(1)} %get-tuple-element.921, ...), kind=kLoop, calls=%fused_computation.240 | loop fusion | flops 28311552 | bytes 4907904 | tf_op jit(solution)/shard_map/convert_element_type | solution.py:105
  44.2 2.2 collective-permute-start.1
  50.8 68.4 %while.35 = (s32[]{:T(128)}, f32[128,2048]{1,0:T(8,128)}, s32[128]{0:T(128)S(1)}, f32[128,2048]{1,0:T(8,128)}, bf16[255,2048]{1,0:T(8,128)(2,1)S(1)}, /*index=5*...) while((s32[]{:T(128)}, f32[128,2048]{1,0:T(8,128)}, ...), condition=%wide.region_4.5_spmd.clone, body=%wide.region_3.4_spmd.clone.sunk | while | flops 17041540 | bytes 10885599 | solution.py:44
  52.8 5.7 %fusion.242 = f32[128,2048]{1,0:T(8,128)} fusion(f32[128,2048]{1,0:T(8,128)} %get-tuple-element.1254, bf16[255,2048]{1,0:T(8,128)(2,1)S(1)} %get-tuple-element.1297, s32[]{:T(128)S(6)} %select_n.2579, f32[2048]{0:T(1024)S(1)} %bitcast.441, s32[]{:T(128)S(6)} %select_n.2596, f32[2048]{0:T(1024)S(1)} %bitcast.442, s32[]{:T(128)S(6)} %select_n.2597, ...), kind=kLoop, calls=%fused_computation.80.clone.1 | loop fusion | flops 17039360 | bytes 10618945 | tf_op jit(solution)/shard_map/while/body/eval_jaxpr/add | solution.py:38
  60.5 6.7 %fusion.242 = f32[128,2048]{1,0:T(8,128)} fusion(f32[128,2048]{1,0:T(8,128)} %get-tuple-element.1254, bf16[255,2048]{1,0:T(8,128)(2,1)S(1)} %get-tuple-element.1297, s32[]{:T(128)S(6)} %select_n.2579, f32[2048]{0:T(1024)S(1)} %bitcast.441, s32[]{:T(128)S(6)} %select_n.2596, f32[2048]{0:T(1024)S(1)} %bitcast.442, s32[]{:T(128)S(6)} %select_n.2597, ...), kind=kLoop, calls=%fused_computation.80.clone.1 | loop fusion | flops 17039360 | bytes 10618945 | tf_op jit(solution)/shard_map/while/body/eval_jaxpr/add | solution.py:38
  69.0 6.7 %fusion.242 = f32[128,2048]{1,0:T(8,128)} fusion(f32[128,2048]{1,0:T(8,128)} %get-tuple-element.1254, bf16[255,2048]{1,0:T(8,128)(2,1)S(1)} %get-tuple-element.1297, s32[]{:T(128)S(6)} %select_n.2579, f32[2048]{0:T(1024)S(1)} %bitcast.441, s32[]{:T(128)S(6)} %select_n.2596, f32[2048]{0:T(1024)S(1)} %bitcast.442, s32[]{:T(128)S(6)} %select_n.2597, ...), kind=kLoop, calls=%fused_computation.80.clone.1 | loop fusion | flops 17039360 | bytes 10618945 | tf_op jit(solution)/shard_map/while/body/eval_jaxpr/add | solution.py:38
  77.8 6.7 %fusion.242 = f32[128,2048]{1,0:T(8,128)} fusion(f32[128,2048]{1,0:T(8,128)} %get-tuple-element.1254, bf16[255,2048]{1,0:T(8,128)(2,1)S(1)} %get-tuple-element.1297, s32[]{:T(128)S(6)} %select_n.2579, f32[2048]{0:T(1024)S(1)} %bitcast.441, s32[]{:T(128)S(6)} %select_n.2596, f32[2048]{0:T(1024)S(1)} %bitcast.442, s32[]{:T(128)S(6)} %select_n.2597, ...), kind=kLoop, calls=%fused_computation.80.clone.1 | loop fusion | flops 17039360 | bytes 10618945 | tf_op jit(solution)/shard_map/while/body/eval_jaxpr/add | solution.py:38
  86.4 6.7 %fusion.242 = f32[128,2048]{1,0:T(8,128)} fusion(f32[128,2048]{1,0:T(8,128)} %get-tuple-element.1254, bf16[255,2048]{1,0:T(8,128)(2,1)S(1)} %get-tuple-element.1297, s32[]{:T(128)S(6)} %select_n.2579, f32[2048]{0:T(1024)S(1)} %bitcast.441, s32[]{:T(128)S(6)} %select_n.2596, f32[2048]{0:T(1024)S(1)} %bitcast.442, s32[]{:T(128)S(6)} %select_n.2597, ...), kind=kLoop, calls=%fused_computation.80.clone.1 | loop fusion | flops 17039360 | bytes 10618945 | tf_op jit(solution)/shard_map/while/body/eval_jaxpr/add | solution.py:38
  95.1 6.7 %fusion.242 = f32[128,2048]{1,0:T(8,128)} fusion(f32[128,2048]{1,0:T(8,128)} %get-tuple-element.1254, bf16[255,2048]{1,0:T(8,128)(2,1)S(1)} %get-tuple-element.1297, s32[]{:T(128)S(6)} %select_n.2579, f32[2048]{0:T(1024)S(1)} %bitcast.441, s32[]{:T(128)S(6)} %select_n.2596, f32[2048]{0:T(1024)S(1)} %bitcast.442, s32[]{:T(128)S(6)} %select_n.2597, ...), kind=kLoop, calls=%fused_computation.80.clone.1 | loop fusion | flops 17039360 | bytes 10618945 | tf_op jit(solution)/shard_map/while/body/eval_jaxpr/add | solution.py:38
  103.7 6.7 %fusion.242 = f32[128,2048]{1,0:T(8,128)} fusion(f32[128,2048]{1,0:T(8,128)} %get-tuple-element.1254, bf16[255,2048]{1,0:T(8,128)(2,1)S(1)} %get-tuple-element.1297, s32[]{:T(128)S(6)} %select_n.2579, f32[2048]{0:T(1024)S(1)} %bitcast.441, s32[]{:T(128)S(6)} %select_n.2596, f32[2048]{0:T(1024)S(1)} %bitcast.442, s32[]{:T(128)S(6)} %select_n.2597, ...), kind=kLoop, calls=%fused_computation.80.clone.1 | loop fusion | flops 17039360 | bytes 10618945 | tf_op jit(solution)/shard_map/while/body/eval_jaxpr/add | solution.py:38
  112.5 6.7 %fusion.242 = f32[128,2048]{1,0:T(8,128)} fusion(f32[128,2048]{1,0:T(8,128)} %get-tuple-element.1254, bf16[255,2048]{1,0:T(8,128)(2,1)S(1)} %get-tuple-element.1297, s32[]{:T(128)S(6)} %select_n.2579, f32[2048]{0:T(1024)S(1)} %bitcast.441, s32[]{:T(128)S(6)} %select_n.2596, f32[2048]{0:T(1024)S(1)} %bitcast.442, s32[]{:T(128)S(6)} %select_n.2597, ...), kind=kLoop, calls=%fused_computation.80.clone.1 | loop fusion | flops 17039360 | bytes 10618945 | tf_op jit(solution)/shard_map/while/body/eval_jaxpr/add | solution.py:38
  119.2 2.1 convolution_bitcast_fusion
  121.5 33.1 %psum.21 = f32[8]{0:T(128)S(1)} all-reduce(f32[8]{0:T(128)S(1)} %convolution_bitcast_fusion.2), channel_id=1, replica_groups=mesh['groups'=2,'ctx'=4,'fsdp'=2,'sub'=2] {'ctx','fsdp','sub'}, use_global_device_ids=true, to_apply=%region_5.6 | all-reduce | flops 8 | bytes 64 | tf_op jit(solution)/shard_map/psum | solution.py:116
  155.0 2.2 fusion.66
  159.8 70.9 %while.34 = (s32[]{:T(128)}, f32[128,2048]{1,0:T(8,128)}, s32[128]{0:T(128)S(1)}, bf16[128,2048]{1,0:T(8,128)(2,1)}, bf16[255,2048]{1,0:T(8,128)(2,1)S(1)}, /*in...) while((s32[]{:T(128)}, f32[128,2048]{1,0:T(8,128)}, ...), condition=%wide.region_48.49_spmd, body=%wide.region_31.48_spmd.sunk | while | flops 17270864 | bytes 10098467 | solution.py:79
  159.9 3.8 fusion.241
  163.7 4.0 %fusion.240 = (f32[2048]{0:T(1024)S(1)}, f32[2048]{0:T(1024)S(1)}, f32[2048]{0:T(1024)S(1)}, f32[2048]{0:T(1024)S(1)}, f32[2048]{0:T(1024)S(1)}, /*index=5*/f32[...) fusion(bf16[128,2048]{1,0:T(8,128)(2,1)} %get-tuple-element.1548, bf16[255,2048]{1,0:T(8,128)(2,1)S(1)} %get-tuple-element.1549, ...), kind=kLoop, calls=%fused_computation.45.clone.1 | loop fusion | flops 8634368 | bytes 4785184 | tf_op jit(solution)/shard_map/while/body/eval_jaxpr/reduce_sum | solution.py:75
  168.8 3.8 fusion.241
  172.6 4.0 %fusion.240 = (f32[2048]{0:T(1024)S(1)}, f32[2048]{0:T(1024)S(1)}, f32[2048]{0:T(1024)S(1)}, f32[2048]{0:T(1024)S(1)}, f32[2048]{0:T(1024)S(1)}, /*index=5*/f32[...) fusion(bf16[128,2048]{1,0:T(8,128)(2,1)} %get-tuple-element.1548, bf16[255,2048]{1,0:T(8,128)(2,1)S(1)} %get-tuple-element.1549, ...), kind=kLoop, calls=%fused_computation.45.clone.1 | loop fusion | flops 8634368 | bytes 4785184 | tf_op jit(solution)/shard_map/while/body/eval_jaxpr/reduce_sum | solution.py:75
  177.6 3.8 fusion.241
  181.5 4.0 %fusion.240 = (f32[2048]{0:T(1024)S(1)}, f32[2048]{0:T(1024)S(1)}, f32[2048]{0:T(1024)S(1)}, f32[2048]{0:T(1024)S(1)}, f32[2048]{0:T(1024)S(1)}, /*index=5*/f32[...) fusion(bf16[128,2048]{1,0:T(8,128)(2,1)} %get-tuple-element.1548, bf16[255,2048]{1,0:T(8,128)(2,1)S(1)} %get-tuple-element.1549, ...), kind=kLoop, calls=%fused_computation.45.clone.1 | loop fusion | flops 8634368 | bytes 4785184 | tf_op jit(solution)/shard_map/while/body/eval_jaxpr/reduce_sum | solution.py:75
  186.5 3.8 fusion.241
  190.3 4.0 %fusion.240 = (f32[2048]{0:T(1024)S(1)}, f32[2048]{0:T(1024)S(1)}, f32[2048]{0:T(1024)S(1)}, f32[2048]{0:T(1024)S(1)}, f32[2048]{0:T(1024)S(1)}, /*index=5*/f32[...) fusion(bf16[128,2048]{1,0:T(8,128)(2,1)} %get-tuple-element.1548, bf16[255,2048]{1,0:T(8,128)(2,1)S(1)} %get-tuple-element.1549, ...), kind=kLoop, calls=%fused_computation.45.clone.1 | loop fusion | flops 8634368 | bytes 4785184 | tf_op jit(solution)/shard_map/while/body/eval_jaxpr/reduce_sum | solution.py:75
  195.4 3.8 fusion.241
  199.2 4.0 %fusion.240 = (f32[2048]{0:T(1024)S(1)}, f32[2048]{0:T(1024)S(1)}, f32[2048]{0:T(1024)S(1)}, f32[2048]{0:T(1024)S(1)}, f32[2048]{0:T(1024)S(1)}, /*index=5*/f32[...) fusion(bf16[128,2048]{1,0:T(8,128)(2,1)} %get-tuple-element.1548, bf16[255,2048]{1,0:T(8,128)(2,1)S(1)} %get-tuple-element.1549, ...), kind=kLoop, calls=%fused_computation.45.clone.1 | loop fusion | flops 8634368 | bytes 4785184 | tf_op jit(solution)/shard_map/while/body/eval_jaxpr/reduce_sum | solution.py:75
  204.2 3.8 fusion.241
  208.1 4.0 %fusion.240 = (f32[2048]{0:T(1024)S(1)}, f32[2048]{0:T(1024)S(1)}, f32[2048]{0:T(1024)S(1)}, f32[2048]{0:T(1024)S(1)}, f32[2048]{0:T(1024)S(1)}, /*index=5*/f32[...) fusion(bf16[128,2048]{1,0:T(8,128)(2,1)} %get-tuple-element.1548, bf16[255,2048]{1,0:T(8,128)(2,1)S(1)} %get-tuple-element.1549, ...), kind=kLoop, calls=%fused_computation.45.clone.1 | loop fusion | flops 8634368 | bytes 4785184 | tf_op jit(solution)/shard_map/while/body/eval_jaxpr/reduce_sum | solution.py:75
  213.1 3.8 fusion.241
  216.9 4.0 %fusion.240 = (f32[2048]{0:T(1024)S(1)}, f32[2048]{0:T(1024)S(1)}, f32[2048]{0:T(1024)S(1)}, f32[2048]{0:T(1024)S(1)}, f32[2048]{0:T(1024)S(1)}, /*index=5*/f32[...) fusion(bf16[128,2048]{1,0:T(8,128)(2,1)} %get-tuple-element.1548, bf16[255,2048]{1,0:T(8,128)(2,1)S(1)} %get-tuple-element.1549, ...), kind=kLoop, calls=%fused_computation.45.clone.1 | loop fusion | flops 8634368 | bytes 4785184 | tf_op jit(solution)/shard_map/while/body/eval_jaxpr/reduce_sum | solution.py:75
  221.9 3.8 fusion.241
  225.8 4.0 %fusion.240 = (f32[2048]{0:T(1024)S(1)}, f32[2048]{0:T(1024)S(1)}, f32[2048]{0:T(1024)S(1)}, f32[2048]{0:T(1024)S(1)}, f32[2048]{0:T(1024)S(1)}, /*index=5*/f32[...) fusion(bf16[128,2048]{1,0:T(8,128)(2,1)} %get-tuple-element.1548, bf16[255,2048]{1,0:T(8,128)(2,1)S(1)} %get-tuple-element.1549, ...), kind=kLoop, calls=%fused_computation.45.clone.1 | loop fusion | flops 8634368 | bytes 4785184 | tf_op jit(solution)/shard_map/while/body/eval_jaxpr/reduce_sum | solution.py:75
  230.7 3.3 fusion.134
  235.4 69.9 %while.36 = (s32[]{:T(128)}, f32[128,2048]{1,0:T(8,128)}, s32[255]{0:T(256)S(1)}, f32[128,2048]{1,0:T(8,128)}, bf16[255,2048]{1,0:T(8,128)(2,1)S(1)}, /*index=5*...) while((s32[]{:T(128)}, f32[128,2048]{1,0:T(8,128)}, ...), condition=%wide.region_8.9_spmd.clone, body=%wide.region_7.8_spmd.clone.sunk | while | flops 17041508 | bytes 10893119 | solution.py:63
  237.5 5.8 %fusion.243 = f32[128,2048]{1,0:T(8,128)} fusion(f32[128,2048]{1,0:T(8,128)} %get-tuple-element.1388, bf16[255,2048]{1,0:T(8,128)(2,1)S(1)} %get-tuple-element.1445, s32[]{:T(128)S(6)} %select_n.2627, f32[2048]{0:T(1024)S(1)} %bitcast.457, s32[]{:T(128)S(6)} %select_n.2644, f32[2048]{0:T(1024)S(1)} %bitcast.458, s32[]{:T(128)S(6)} %select_n.2645, ...), kind=kLoop, calls=%fused_computation.128.clone.1 | loop fusion | flops 17039360 | bytes 10618945 | tf_op jit(solution)/shard_map/while/body/eval_jaxpr/add | solution.py:57
  245.4 6.8 %fusion.243 = f32[128,2048]{1,0:T(8,128)} fusion(f32[128,2048]{1,0:T(8,128)} %get-tuple-element.1388, bf16[255,2048]{1,0:T(8,128)(2,1)S(1)} %get-tuple-element.1445, s32[]{:T(128)S(6)} %select_n.2627, f32[2048]{0:T(1024)S(1)} %bitcast.457, s32[]{:T(128)S(6)} %select_n.2644, f32[2048]{0:T(1024)S(1)} %bitcast.458, s32[]{:T(128)S(6)} %select_n.2645, ...), kind=kLoop, calls=%fused_computation.128.clone.1 | loop fusion | flops 17039360 | bytes 10618945 | tf_op jit(solution)/shard_map/while/body/eval_jaxpr/add | solution.py:57
  254.1 6.8 %fusion.243 = f32[128,2048]{1,0:T(8,128)} fusion(f32[128,2048]{1,0:T(8,128)} %get-tuple-element.1388, bf16[255,2048]{1,0:T(8,128)(2,1)S(1)} %get-tuple-element.1445, s32[]{:T(128)S(6)} %select_n.2627, f32[2048]{0:T(1024)S(1)} %bitcast.457, s32[]{:T(128)S(6)} %select_n.2644, f32[2048]{0:T(1024)S(1)} %bitcast.458, s32[]{:T(128)S(6)} %select_n.2645, ...), kind=kLoop, calls=%fused_computation.128.clone.1 | loop fusion | flops 17039360 | bytes 10618945 | tf_op jit(solution)/shard_map/while/body/eval_jaxpr/add | solution.py:57
  263.1 6.8 %fusion.243 = f32[128,2048]{1,0:T(8,128)} fusion(f32[128,2048]{1,0:T(8,128)} %get-tuple-element.1388, bf16[255,2048]{1,0:T(8,128)(2,1)S(1)} %get-tuple-element.1445, s32[]{:T(128)S(6)} %select_n.2627, f32[2048]{0:T(1024)S(1)} %bitcast.457, s32[]{:T(128)S(6)} %select_n.2644, f32[2048]{0:T(1024)S(1)} %bitcast.458, s32[]{:T(128)S(6)} %select_n.2645, ...), kind=kLoop, calls=%fused_computation.128.clone.1 | loop fusion | flops 17039360 | bytes 10618945 | tf_op jit(solution)/shard_map/while/body/eval_jaxpr/add | solution.py:57
  271.8 6.8 %fusion.243 = f32[128,2048]{1,0:T(8,128)} fusion(f32[128,2048]{1,0:T(8,128)} %get-tuple-element.1388, bf16[255,2048]{1,0:T(8,128)(2,1)S(1)} %get-tuple-element.1445, s32[]{:T(128)S(6)} %select_n.2627, f32[2048]{0:T(1024)S(1)} %bitcast.457, s32[]{:T(128)S(6)} %select_n.2644, f32[2048]{0:T(1024)S(1)} %bitcast.458, s32[]{:T(128)S(6)} %select_n.2645, ...), kind=kLoop, calls=%fused_computation.128.clone.1 | loop fusion | flops 17039360 | bytes 10618945 | tf_op jit(solution)/shard_map/while/body/eval_jaxpr/add | solution.py:57
  280.8 6.8 %fusion.243 = f32[128,2048]{1,0:T(8,128)} fusion(f32[128,2048]{1,0:T(8,128)} %get-tuple-element.1388, bf16[255,2048]{1,0:T(8,128)(2,1)S(1)} %get-tuple-element.1445, s32[]{:T(128)S(6)} %select_n.2627, f32[2048]{0:T(1024)S(1)} %bitcast.457, s32[]{:T(128)S(6)} %select_n.2644, f32[2048]{0:T(1024)S(1)} %bitcast.458, s32[]{:T(128)S(6)} %select_n.2645, ...), kind=kLoop, calls=%fused_computation.128.clone.1 | loop fusion | flops 17039360 | bytes 10618945 | tf_op jit(solution)/shard_map/while/body/eval_jaxpr/add | solution.py:57
  289.5 6.8 %fusion.243 = f32[128,2048]{1,0:T(8,128)} fusion(f32[128,2048]{1,0:T(8,128)} %get-tuple-element.1388, bf16[255,2048]{1,0:T(8,128)(2,1)S(1)} %get-tuple-element.1445, s32[]{:T(128)S(6)} %select_n.2627, f32[2048]{0:T(1024)S(1)} %bitcast.457, s32[]{:T(128)S(6)} %select_n.2644, f32[2048]{0:T(1024)S(1)} %bitcast.458, s32[]{:T(128)S(6)} %select_n.2645, ...), kind=kLoop, calls=%fused_computation.128.clone.1 | loop fusion | flops 17039360 | bytes 10618945 | tf_op jit(solution)/shard_map/while/body/eval_jaxpr/add | solution.py:57
  296.2 1.9 constant_dynamic-slice_fusion.36
  298.5 6.8 %fusion.243 = f32[128,2048]{1,0:T(8,128)} fusion(f32[128,2048]{1,0:T(8,128)} %get-tuple-element.1388, bf16[255,2048]{1,0:T(8,128)(2,1)S(1)} %get-tuple-element.1445, s32[]{:T(128)S(6)} %select_n.2627, f32[2048]{0:T(1024)S(1)} %bitcast.457, s32[]{:T(128)S(6)} %select_n.2644, f32[2048]{0:T(1024)S(1)} %bitcast.458, s32[]{:T(128)S(6)} %select_n.2645, ...), kind=kLoop, calls=%fused_computation.128.clone.1 | loop fusion | flops 17039360 | bytes 10618945 | tf_op jit(solution)/shard_map/while/body/eval_jaxpr/add | solution.py:57
  305.3 3.1 fusion.155
  311.8 2.0 fusion.157
  314.7 2.7 fusion.178
  326.4 52.9 %all-reduce.3.cloned.1.call-done = (f32[3,7,2048]{2,1,0:T(8,128)}, f32[128,2048]{1,0:T(8,128)}) async-done(((f32[3,7,2048]{2,1,0:T(8,128)}, f32[128,2048]{1,0:T(8,128)}), (f32[3,7,2048]{2,1,0:T(8,128)}, f32[128,2048]{1,0:T(8,128)})) %all-reduce.3.cloned.1.call-update) | async-done | bytes 1220624 | tf_op jit(solution)/shard_map/psum | solution.py:138
  (247 shorter events, 67.3 us)
Async XLA Ops:
  7.2 372.2 %all-reduce.3.cloned.1.call-start = ((), (), s32[]{:S(2)}) async-start(), calls=%async_computation | async-start | bytes 2490368 | tf_op jit(solution)/shard_map/psum | solution.py:138
  8.1 25.3 %collective-permute-start = (bf16[3,6,2048]{2,1,0:T(8,128)(2,1)S(1)}, bf16[3,6,2048]{2,1,0:T(8,128)(2,1)S(1)}, u32[]{:S(2)}, u32[]{:S(2)}) collective-permute-start(bf16[3,6,2048]{2,1,0:T(8,128)(2,1)S(1)} %slice.171), channel_id=1, source_target_pairs={{0,1},{1,4},{4,5},{5,8},{8,9},{9,12},{12,13},{2,3},{3,6},{6,7},{7,... | collective-permute-start | bytes 221192 | tf_op jit(solution)/shard_map/ppermute | solution.py:14
  12.4 30.8 %copy-start.10 = (f32[1,1,2048]{2,1,0:T(1,128)}, f32[1,1,2048]{2,1,0:T(1,128)S(1)}, u32[]{:S(2)}) copy-start(f32[1,1,2048]{2,1,0:T(1,128)S(1)} %get-tuple-element.899) | copy-start | bytes 24580
  12.4 30.8 %copy-start.12 = (f32[1,1,2048]{2,1,0:T(1,128)}, f32[1,1,2048]{2,1,0:T(1,128)S(1)}, u32[]{:S(2)}) copy-start(f32[1,1,2048]{2,1,0:T(1,128)S(1)} %get-tuple-element.900) | copy-start | bytes 24580
  12.4 30.8 %copy-start.14 = (f32[1,1,2048]{2,1,0:T(1,128)}, f32[1,1,2048]{2,1,0:T(1,128)S(1)}, u32[]{:S(2)}) copy-start(f32[1,1,2048]{2,1,0:T(1,128)S(1)} %get-tuple-element.901) | copy-start | bytes 24580
  12.4 30.8 %copy-start.16 = (f32[1,1,2048]{2,1,0:T(1,128)}, f32[1,1,2048]{2,1,0:T(1,128)S(1)}, u32[]{:S(2)}) copy-start(f32[1,1,2048]{2,1,0:T(1,128)S(1)} %get-tuple-element.902) | copy-start | bytes 24580
  12.4 30.8 %copy-start.18 = (f32[1,1,2048]{2,1,0:T(1,128)}, f32[1,1,2048]{2,1,0:T(1,128)S(1)}, u32[]{:S(2)}) copy-start(f32[1,1,2048]{2,1,0:T(1,128)S(1)} %get-tuple-element.903) | copy-start | bytes 24580
  12.4 30.8 %copy-start.20 = (f32[1,1,2048]{2,1,0:T(1,128)}, f32[1,1,2048]{2,1,0:T(1,128)S(1)}, u32[]{:S(2)}) copy-start(f32[1,1,2048]{2,1,0:T(1,128)S(1)} %get-tuple-element.904) | copy-start | bytes 24580
  12.5 30.8 %copy-start.22 = (f32[1,1,2048]{2,1,0:T(1,128)}, f32[1,1,2048]{2,1,0:T(1,128)S(1)}, u32[]{:S(2)}) copy-start(f32[1,1,2048]{2,1,0:T(1,128)S(1)} %get-tuple-element.905) | copy-start | bytes 24580
  12.5 30.8 %copy-start.24 = (f32[1,1,2048]{2,1,0:T(1,128)}, f32[1,1,2048]{2,1,0:T(1,128)S(1)}, u32[]{:S(2)}) copy-start(f32[1,1,2048]{2,1,0:T(1,128)S(1)} %get-tuple-element.906) | copy-start | bytes 24580
  12.5 35.2 %copy-start.26 = (f32[1,1,2048]{2,1,0:T(1,128)}, f32[1,1,2048]{2,1,0:T(1,128)S(1)}, u32[]{:S(2)}) copy-start(f32[1,1,2048]{2,1,0:T(1,128)S(1)} %get-tuple-element.894) | copy-start | bytes 24580
  12.5 35.2 %copy-start.28 = (f32[1,1,2048]{2,1,0:T(1,128)}, f32[1,1,2048]{2,1,0:T(1,128)S(1)}, u32[]{:S(2)}) copy-start(f32[1,1,2048]{2,1,0:T(1,128)S(1)} %get-tuple-element.907) | copy-start | bytes 24580
  12.5 35.2 %copy-start.30 = (f32[1,1,2048]{2,1,0:T(1,128)}, f32[1,1,2048]{2,1,0:T(1,128)S(1)}, u32[]{:S(2)}) copy-start(f32[1,1,2048]{2,1,0:T(1,128)S(1)} %get-tuple-element.908) | copy-start | bytes 24580
  12.5 35.2 %copy-start.32 = (f32[1,1,2048]{2,1,0:T(1,128)}, f32[1,1,2048]{2,1,0:T(1,128)S(1)}, u32[]{:S(2)}) copy-start(f32[1,1,2048]{2,1,0:T(1,128)S(1)} %get-tuple-element.909) | copy-start | bytes 24580
  12.5 35.2 %copy-start.34 = (f32[1,1,2048]{2,1,0:T(1,128)}, f32[1,1,2048]{2,1,0:T(1,128)S(1)}, u32[]{:S(2)}) copy-start(f32[1,1,2048]{2,1,0:T(1,128)S(1)} %get-tuple-element.910) | copy-start | bytes 24580
  12.5 35.2 %copy-start.36 = (f32[1,1,2048]{2,1,0:T(1,128)}, f32[1,1,2048]{2,1,0:T(1,128)S(1)}, u32[]{:S(2)}) copy-start(f32[1,1,2048]{2,1,0:T(1,128)S(1)} %get-tuple-element.911) | copy-start | bytes 24580
  12.5 35.2 %copy-start.38 = (f32[1,1,2048]{2,1,0:T(1,128)}, f32[1,1,2048]{2,1,0:T(1,128)S(1)}, u32[]{:S(2)}) copy-start(f32[1,1,2048]{2,1,0:T(1,128)S(1)} %get-tuple-element.912) | copy-start | bytes 24580
  13.5 29.7 %copy-start.40 = (f32[1,1,2048]{2,1,0:T(1,128)}, f32[1,1,2048]{2,1,0:T(1,128)S(1)}, u32[]{:S(2)}) copy-start(f32[1,1,2048]{2,1,0:T(1,128)S(1)} %get-tuple-element.913) | copy-start | bytes 24580
  13.5 29.7 %copy-start.42 = (f32[1,1,2048]{2,1,0:T(1,128)}, f32[1,1,2048]{2,1,0:T(1,128)S(1)}, u32[]{:S(2)}) copy-start(f32[1,1,2048]{2,1,0:T(1,128)S(1)} %get-tuple-element.914) | copy-start | bytes 24580
  15.1 31.4 %copy-start.7 = (s32[255]{0:T(256)}, s32[255]{0:T(256)S(1)}, u32[]{:S(2)}) copy-start(s32[255]{0:T(256)S(1)} %fusion.225) | copy-start | bytes 3064
  15.8 31.9 %copy-start.47 = (pred[128]{0:T(512)(128)(4,1)}, pred[128]{0:T(512)(128)(4,1)S(1)}, u32[]{:S(2)}) copy-start(pred[128]{0:T(512)(128)(4,1)S(1)} %get-tuple-element.922) | copy-start | bytes 388
  15.8 31.9 %copy-start.49 = (pred[128]{0:T(512)(128)(4,1)}, pred[128]{0:T(512)(128)(4,1)S(1)}, u32[]{:S(2)}) copy-start(pred[128]{0:T(512)(128)(4,1)S(1)} %get-tuple-element.917) | copy-start | bytes 388
  15.8 31.9 %copy-start.51 = (pred[128]{0:T(512)(128)(4,1)}, pred[128]{0:T(512)(128)(4,1)S(1)}, u32[]{:S(2)}) copy-start(pred[128]{0:T(512)(128)(4,1)S(1)} %get-tuple-element.918) | copy-start | bytes 388
  15.8 31.9 %copy-start.53 = (pred[128]{0:T(512)(128)(4,1)}, pred[128]{0:T(512)(128)(4,1)S(1)}, u32[]{:S(2)}) copy-start(pred[128]{0:T(512)(128)(4,1)S(1)} %get-tuple-element.919) | copy-start | bytes 388
  15.8 31.9 %copy-start.55 = (pred[128]{0:T(512)(128)(4,1)}, pred[128]{0:T(512)(128)(4,1)S(1)}, u32[]{:S(2)}) copy-start(pred[128]{0:T(512)(128)(4,1)S(1)} %get-tuple-element.920) | copy-start | bytes 388
  15.8 31.9 %copy-start.57 = (pred[128]{0:T(512)(128)(4,1)}, pred[128]{0:T(512)(128)(4,1)S(1)}, u32[]{:S(2)}) copy-start(pred[128]{0:T(512)(128)(4,1)S(1)} %get-tuple-element.921) | copy-start | bytes 388
  33.4 12.9 %copy-start.67 = (s32[8]{0:T(128)S(1)}, s32[8]{0:T(128)}, u32[]{:S(2)}) copy-start(s32[8]{0:T(128)} %param.19) | copy-start | bytes 100
  43.3 4.5 %copy-start = (bf16[3,128,2048]{2,1,0:T(8,128)(2,1)S(1)}, bf16[3,128,2048]{2,1,0:T(8,128)(2,1)}, u32[]{:S(2)}) copy-start(bf16[3,128,2048]{2,1,0:T(8,128)(2,1)} %param.13) | copy-start | bytes 4718596
  44.2 5.4 %collective-permute-start.1 = (bf16[127,2048]{1,0:T(8,128)(2,1)S(1)}, bf16[127,2048]{1,0:T(8,128)(2,1)}, u32[]{:S(2)}, u32[]{:S(2)}) collective-permute-start(bf16[127,2048]{1,0:T(8,128)(2,1)S(1)} %slice.175), channel_id=1, source_target_pairs={{0,1},{1,4},{4,5},{5,8},{8,9},{9,12},{12,13},{2,3},{3,6},{6,7},{7,... | collective-permute-start | bytes 1560584 | tf_op jit(solution)/shard_map/ppermute | solution.py:14
  50.8 68.4 %copy-start.9 = (f32[2048]{0:T(1024)S(1)}, f32[2048]{0:T(1024)}, u32[]{:S(2)}) copy-start(f32[2048]{0:T(1024)} %param.17) | copy-start | bytes 24580
  50.8 103.8 %copy-start.66 = (s32[8]{0:T(128)S(1)}, s32[8]{0:T(128)}, u32[]{:S(2)}) copy-start(s32[8]{0:T(128)} %param.18) | copy-start | bytes 100
  50.8 103.8 %copy-start.68 = (s32[8]{0:T(128)S(1)}, s32[8]{0:T(128)}, u32[]{:S(2)}) copy-start(s32[8]{0:T(128)} %param.19) | copy-start | bytes 100
  155.0 4.8 %copy-start.65 = (f32[128]{0:T(128)}, f32[128]{0:T(128)S(1)}, u32[]{:S(2)}) copy-start(f32[128]{0:T(128)S(1)} %convolution_bitcast_fusion.1) | copy-start | bytes 1540
  157.2 76.8 %collective-permute-start.2 = (bf16[127,2048]{1,0:T(8,128)(2,1)}, bf16[127,2048]{1,0:T(8,128)(2,1)}, u32[]{:S(2)}, u32[]{:S(2)}) collective-permute-start(bf16[127,2048]{1,0:T(8,128)(2,1)} %bitcast.321), channel_id=1, source_target_pairs={{1,0},{4,1},{5,4},{8,5},{9,8},{12,9},{13,12},{3,2},{6,3},{7,6},{10... | collective-permute-start | bytes 1560584 | tf_op jit(solution)/shard_map/ppermute | solution.py:14
  159.8 71.0 %copy-start.4 = (bf16[128,2048]{1,0:T(8,128)(2,1)S(1)}, bf16[128,2048]{1,0:T(8,128)(2,1)}, u32[]{:S(2)}) copy-start(bf16[128,2048]{1,0:T(8,128)(2,1)} %param.16) | copy-start | bytes 1572868
  235.4 69.9 %copy-start.56 = (pred[128]{0:T(512)(128)(4,1)S(1)}, pred[128]{0:T(512)(128)(4,1)}, u32[]{:S(2)}) copy-start(pred[128]{0:T(512)(128)(4,1)} %copy-done.55) | copy-start | bytes 388
  235.4 69.9 %copy-start.58 = (pred[128]{0:T(512)(128)(4,1)S(1)}, pred[128]{0:T(512)(128)(4,1)}, u32[]{:S(2)}) copy-start(pred[128]{0:T(512)(128)(4,1)} %copy-done.57) | copy-start | bytes 388
  305.2 3.2 copy-start.1
  305.2 3.2 copy-start.5
  305.3 3.2 copy-start.6
  305.3 3.1 copy-start.48
  309.5 2.2 copy-start.44
  309.5 2.3 copy-start.50
  309.5 2.3 copy-start.52
  309.5 2.3 copy-start.54
  310.2 8.9 %collective-permute-start.3 = (bf16[3,6,2048]{2,1,0:T(8,128)(2,1)}, bf16[3,6,2048]{2,1,0:T(8,128)(2,1)S(1)}, u32[]{:S(2)}, u32[]{:S(2)}) collective-permute-start(bf16[3,6,2048]{2,1,0:T(8,128)(2,1)} %pad_maximum_fusion.6), channel_id=1, source_target_pairs={{1,0},{4,1},{5,4},{8,5},{9,8},{12,9},{13,12},{3,2},{6,3},{7,6},{10... | collective-permute-start | bytes 221192 | tf_op jit(solution)/shard_map/ppermute | solution.py:14
  313.8 3.6 copy-start.45
  313.8 3.6 copy-start.46
  (27 other events, 32.2 us)
Sparse Core Ops, SparseCore 0:
  319.0 60.2 all-reduce.2
where the time goes:
time: 392 us; the launch traced here: 389 us
  other arithmetic  210 us (54%)
  waiting for transfers between devices  52.9 us (13%)
  blocking collectives  50.7 us (13%)
  local copies, waits for them, and re-layouts  46.6 us (12%)
  between operations  15 us (4%)
  starting transfers between devices  7.57 us (2%)
    reduce_sum x21, other arithmetic, correlate_advance(): jnp.sum(jnp.where((row_age >= j)[:, None], product, 0.0), axis=0)  74.8 us
    add x8, other arithmetic, reverse_advance(): running + jnp.where(keep[:, None], weight_row[None, :] * window.astype(jn...  53.1 us
    psum x1, waiting for transfers between devices, local(): filter_all, d_feat = lax.psum((filter_part, taps_part), ('ctx', 'sub'))  52.9 us
    add x8, other arithmetic, causal_advance(): running + jnp.where((row_age >= j)[:, None], weight_row[None, :] * window...  52.7 us
    psum x1, blocking collectives, local(): totals = lax.psum(partial_sums, ('ctx', 'fsdp', 'sub'))  33.1 us
    all_gather x1, blocking collectives, local(): lax.all_gather(long_filter, 'ctx', axis=0, tiled=True).astype(jnp.float32)  17.6 us
    dynamic_slice x9, local copies, waits for them, and re-layouts, reverse_advance(): weight_row = lax.dynamic_index_in_dim(tap_table, j, 0, keepdims=False)  15.9 us
    dynamic_slice x9, local copies, waits for them, and re-layouts, causal_advance(): weight_row = lax.dynamic_index_in_dim(tap_table, j, 0, keepdims=False)  15 us
  transfers between devices with their start and end apart: 5, of which 1 were waited for; matrix products, arithmetic and copies ran while one was open for 25% of the time, Pallas kernels for 0%

commit v1 on v0

--- a/solution.py
+++ b/solution.py
@@ -113,7 +113,7 @@
         jnp.float32
     )
     partial_sums = jnp.dot(projected, onehot, precision=HIGH)
-    totals = lax.psum(partial_sums, ("ctx", "fsdp", "sub"))
+    totals = jnp.sum(lax.all_gather(partial_sums, ("ctx", "fsdp", "sub")), axis=0)
     coef = list_coef(totals, seg_lengths, list_ids)
     tok_coef = jnp.dot(onehot, coef, precision=HIGH)
     d_out = upstream.astype(jnp.float32) + tok_coef[:, None] * score_dir[None, :]

time: 392 us -> 393 us (level)
    psum x1 -> x0, blocking collectives: 33.1 us -> none  [local(): totals = lax.psum(partial_sums, ('ctx', 'fsdp', 'sub'))]
    unnamed x0 -> x1, blocking collectives: none -> 31.4 us
where the time goes in v1:
time: 393 us; the launch traced here: 390 us
  other arithmetic  211 us (54%)
  waiting for transfers between devices  52.9 us (13%)
  blocking collectives  49 us (12%)
  local copies, waits for them, and re-layouts  48 us (12%)
  between operations  15.6 us (4%)
  starting transfers between devices  7.57 us (2%)
    reduce_sum x21, other arithmetic, correlate_advance(): jnp.sum(jnp.where((row_age >= j)[:, None], product, 0.0), axis=0)  74.8 us
    add x8, other arithmetic, reverse_advance(): running + jnp.where(keep[:, None], weight_row[None, :] * window.astype(jn...  53.1 us
    psum x1, waiting for transfers between devices, local(): filter_all, d_feat = lax.psum((filter_part, taps_part), ('ctx', 'sub'))  52.9 us
    add x8, other arithmetic, causal_advance(): running + jnp.where((row_age >= j)[:, None], weight_row[None, :] * window...  52.7 us
    unnamed x1, blocking collectives  31.4 us
    all_gather x1, blocking collectives, local(): lax.all_gather(long_filter, 'ctx', axis=0, tiled=True).astype(jnp.float32)  17.6 us
    dynamic_slice x9, local copies, waits for them, and re-layouts, reverse_advance(): weight_row = lax.dynamic_index_in_dim(tap_table, j, 0, keepdims=False)  15.9 us
    dynamic_slice x9, local copies, waits for them, and re-layouts, causal_advance(): weight_row = lax.dynamic_index_in_dim(tap_table, j, 0, keepdims=False)  15 us
  transfers between devices with their start and end apart: 5, of which 1 were waited for; matrix products, arithmetic and copies ran while one was open for 25% of the time, Pallas kernels for 0%

profile of v1, /device:TPU:0, one launch (start us, length us, event | category | flops | bytes accessed | tf_op | source)
XLA Modules:
  0.0 390.0 jit_solution(6260261182069316988)
XLA Ops:
  8.1 2.4 collective-permute-start
  15.9 17.6 %all_gather.9 = bf16[128,2048]{1,0:T(8,128)(2,1)S(1)} all-gather(bf16[32,2048]{1,0:T(8,128)(2,1)} %param.15), channel_id=1, replica_groups=mesh['groups'=2,'ctx'=4,'fsdp'=2,'sub'=2] {'ctx'}, dimensions={0}, use_global_device_ids=true | all-gather | bytes 655360 | tf_op jit(solution)/shard_map/all_gather | solution.py:106
  33.4 9.7 %fusion.68 = (bf16[128,2048]{1,0:T(8,128)(2,1)S(1)}, bf16[128,2048]{1,0:T(8,128)(2,1)}, bf16[128,2048]{1,0:T(8,128)(2,1)}, bf16[128,2048]{1,0:T(8,128)(2,1)}) fusion(f32[2048]{0:T(1024)S(1)} %bitcast.487, pred[128]{0:T(512)(128)(4,1)S(1)} %get-tuple-element.922, f32[2048]{0:T(1024)S(1)} %bitcast.489, pred[128]{0:T(512)(128)(4,1)S(1)} %get-tuple-element.921, ...), kind=kLoop, calls=%fused_computation.240 | loop fusion | flops 28311552 | bytes 4907904 | tf_op jit(solution)/shard_map/convert_element_type | solution.py:105
  44.2 2.2 collective-permute-start.1
  52.6 68.4 %while.35 = (s32[]{:T(128)}, f32[128,2048]{1,0:T(8,128)}, s32[128]{0:T(128)S(1)}, f32[128,2048]{1,0:T(8,128)}, bf16[255,2048]{1,0:T(8,128)(2,1)S(1)}, /*index=5*...) while((s32[]{:T(128)}, f32[128,2048]{1,0:T(8,128)}, ...), condition=%wide.region_4.5_spmd.clone, body=%wide.region_3.4_spmd.clone.sunk | while | flops 17041540 | bytes 10885599 | solution.py:44
  54.6 5.7 %fusion.242 = f32[128,2048]{1,0:T(8,128)} fusion(f32[128,2048]{1,0:T(8,128)} %get-tuple-element.1254, bf16[255,2048]{1,0:T(8,128)(2,1)S(1)} %get-tuple-element.1297, s32[]{:T(128)S(6)} %select_n.2579, f32[2048]{0:T(1024)S(1)} %bitcast.442, s32[]{:T(128)S(6)} %select_n.2596, f32[2048]{0:T(1024)S(1)} %bitcast.443, s32[]{:T(128)S(6)} %select_n.2597, ...), kind=kLoop, calls=%fused_computation.80.clone.1 | loop fusion | flops 17039360 | bytes 10618945 | tf_op jit(solution)/shard_map/while/body/eval_jaxpr/add | solution.py:38
  62.3 6.7 %fusion.242 = f32[128,2048]{1,0:T(8,128)} fusion(f32[128,2048]{1,0:T(8,128)} %get-tuple-element.1254, bf16[255,2048]{1,0:T(8,128)(2,1)S(1)} %get-tuple-element.1297, s32[]{:T(128)S(6)} %select_n.2579, f32[2048]{0:T(1024)S(1)} %bitcast.442, s32[]{:T(128)S(6)} %select_n.2596, f32[2048]{0:T(1024)S(1)} %bitcast.443, s32[]{:T(128)S(6)} %select_n.2597, ...), kind=kLoop, calls=%fused_computation.80.clone.1 | loop fusion | flops 17039360 | bytes 10618945 | tf_op jit(solution)/shard_map/while/body/eval_jaxpr/add | solution.py:38
  70.8 6.7 %fusion.242 = f32[128,2048]{1,0:T(8,128)} fusion(f32[128,2048]{1,0:T(8,128)} %get-tuple-element.1254, bf16[255,2048]{1,0:T(8,128)(2,1)S(1)} %get-tuple-element.1297, s32[]{:T(128)S(6)} %select_n.2579, f32[2048]{0:T(1024)S(1)} %bitcast.442, s32[]{:T(128)S(6)} %select_n.2596, f32[2048]{0:T(1024)S(1)} %bitcast.443, s32[]{:T(128)S(6)} %select_n.2597, ...), kind=kLoop, calls=%fused_computation.80.clone.1 | loop fusion | flops 17039360 | bytes 10618945 | tf_op jit(solution)/shard_map/while/body/eval_jaxpr/add | solution.py:38
  79.6 6.7 %fusion.242 = f32[128,2048]{1,0:T(8,128)} fusion(f32[128,2048]{1,0:T(8,128)} %get-tuple-element.1254, bf16[255,2048]{1,0:T(8,128)(2,1)S(1)} %get-tuple-element.1297, s32[]{:T(128)S(6)} %select_n.2579, f32[2048]{0:T(1024)S(1)} %bitcast.442, s32[]{:T(128)S(6)} %select_n.2596, f32[2048]{0:T(1024)S(1)} %bitcast.443, s32[]{:T(128)S(6)} %select_n.2597, ...), kind=kLoop, calls=%fused_computation.80.clone.1 | loop fusion | flops 17039360 | bytes 10618945 | tf_op jit(solution)/shard_map/while/body/eval_jaxpr/add | solution.py:38
  88.1 6.7 %fusion.242 = f32[128,2048]{1,0:T(8,128)} fusion(f32[128,2048]{1,0:T(8,128)} %get-tuple-element.1254, bf16[255,2048]{1,0:T(8,128)(2,1)S(1)} %get-tuple-element.1297, s32[]{:T(128)S(6)} %select_n.2579, f32[2048]{0:T(1024)S(1)} %bitcast.442, s32[]{:T(128)S(6)} %select_n.2596, f32[2048]{0:T(1024)S(1)} %bitcast.443, s32[]{:T(128)S(6)} %select_n.2597, ...), kind=kLoop, calls=%fused_computation.80.clone.1 | loop fusion | flops 17039360 | bytes 10618945 | tf_op jit(solution)/shard_map/while/body/eval_jaxpr/add | solution.py:38
  96.9 6.7 %fusion.242 = f32[128,2048]{1,0:T(8,128)} fusion(f32[128,2048]{1,0:T(8,128)} %get-tuple-element.1254, bf16[255,2048]{1,0:T(8,128)(2,1)S(1)} %get-tuple-element.1297, s32[]{:T(128)S(6)} %select_n.2579, f32[2048]{0:T(1024)S(1)} %bitcast.442, s32[]{:T(128)S(6)} %select_n.2596, f32[2048]{0:T(1024)S(1)} %bitcast.443, s32[]{:T(128)S(6)} %select_n.2597, ...), kind=kLoop, calls=%fused_computation.80.clone.1 | loop fusion | flops 17039360 | bytes 10618945 | tf_op jit(solution)/shard_map/while/body/eval_jaxpr/add | solution.py:38
  105.4 6.7 %fusion.242 = f32[128,2048]{1,0:T(8,128)} fusion(f32[128,2048]{1,0:T(8,128)} %get-tuple-element.1254, bf16[255,2048]{1,0:T(8,128)(2,1)S(1)} %get-tuple-element.1297, s32[]{:T(128)S(6)} %select_n.2579, f32[2048]{0:T(1024)S(1)} %bitcast.442, s32[]{:T(128)S(6)} %select_n.2596, f32[2048]{0:T(1024)S(1)} %bitcast.443, s32[]{:T(128)S(6)} %select_n.2597, ...), kind=kLoop, calls=%fused_computation.80.clone.1 | loop fusion | flops 17039360 | bytes 10618945 | tf_op jit(solution)/shard_map/while/body/eval_jaxpr/add | solution.py:38
  112.2 1.9 constant_dynamic-slice_fusion.35
  114.2 6.7 %fusion.242 = f32[128,2048]{1,0:T(8,128)} fusion(f32[128,2048]{1,0:T(8,128)} %get-tuple-element.1254, bf16[255,2048]{1,0:T(8,128)(2,1)S(1)} %get-tuple-element.1297, s32[]{:T(128)S(6)} %select_n.2579, f32[2048]{0:T(1024)S(1)} %bitcast.442, s32[]{:T(128)S(6)} %select_n.2596, f32[2048]{0:T(1024)S(1)} %bitcast.443, s32[]{:T(128)S(6)} %select_n.2597, ...), kind=kLoop, calls=%fused_computation.80.clone.1 | loop fusion | flops 17039360 | bytes 10618945 | tf_op jit(solution)/shard_map/while/body/eval_jaxpr/add | solution.py:38
  121.0 2.2 convolution_bitcast_fusion
  123.6 31.4 %all-reduce = f32[128]{0:T(128)S(1)} all-reduce(f32[128]{0:T(128)S(1)} %dynamic-update-slice), channel_id=2, replica_groups=mesh['groups'=2,'ctx'=4,'fsdp'=2,'sub'=2] {'ctx','fsdp','sub'}, use_global_device_ids=true, to_apply=%add | all-reduce | flops 128 | bytes 1024
  155.5 2.2 fusion.66
  160.3 71.0 %while.34 = (s32[]{:T(128)}, f32[128,2048]{1,0:T(8,128)}, s32[128]{0:T(128)S(1)}, bf16[128,2048]{1,0:T(8,128)(2,1)}, bf16[255,2048]{1,0:T(8,128)(2,1)S(1)}, /*in...) while((s32[]{:T(128)}, f32[128,2048]{1,0:T(8,128)}, ...), condition=%wide.region_48.49_spmd, body=%wide.region_31.48_spmd.sunk | while | flops 17270864 | bytes 10098467 | solution.py:79
  160.4 3.8 fusion.241
  164.2 4.0 %fusion.240 = (f32[2048]{0:T(1024)S(1)}, f32[2048]{0:T(1024)S(1)}, f32[2048]{0:T(1024)S(1)}, f32[2048]{0:T(1024)S(1)}, f32[2048]{0:T(1024)S(1)}, /*index=5*/f32[...) fusion(bf16[128,2048]{1,0:T(8,128)(2,1)} %get-tuple-element.1548, bf16[255,2048]{1,0:T(8,128)(2,1)S(1)} %get-tuple-element.1549, ...), kind=kLoop, calls=%fused_computation.45.clone.1 | loop fusion | flops 8634368 | bytes 4785184 | tf_op jit(solution)/shard_map/while/body/eval_jaxpr/reduce_sum | solution.py:75
  169.3 3.8 fusion.241
  173.1 4.0 %fusion.240 = (f32[2048]{0:T(1024)S(1)}, f32[2048]{0:T(1024)S(1)}, f32[2048]{0:T(1024)S(1)}, f32[2048]{0:T(1024)S(1)}, f32[2048]{0:T(1024)S(1)}, /*index=5*/f32[...) fusion(bf16[128,2048]{1,0:T(8,128)(2,1)} %get-tuple-element.1548, bf16[255,2048]{1,0:T(8,128)(2,1)S(1)} %get-tuple-element.1549, ...), kind=kLoop, calls=%fused_computation.45.clone.1 | loop fusion | flops 8634368 | bytes 4785184 | tf_op jit(solution)/shard_map/while/body/eval_jaxpr/reduce_sum | solution.py:75
  178.1 3.8 fusion.241
  182.0 4.0 %fusion.240 = (f32[2048]{0:T(1024)S(1)}, f32[2048]{0:T(1024)S(1)}, f32[2048]{0:T(1024)S(1)}, f32[2048]{0:T(1024)S(1)}, f32[2048]{0:T(1024)S(1)}, /*index=5*/f32[...) fusion(bf16[128,2048]{1,0:T(8,128)(2,1)} %get-tuple-element.1548, bf16[255,2048]{1,0:T(8,128)(2,1)S(1)} %get-tuple-element.1549, ...), kind=kLoop, calls=%fused_computation.45.clone.1 | loop fusion | flops 8634368 | bytes 4785184 | tf_op jit(solution)/shard_map/while/body/eval_jaxpr/reduce_sum | solution.py:75
  187.0 3.8 fusion.241
  190.8 4.0 %fusion.240 = (f32[2048]{0:T(1024)S(1)}, f32[2048]{0:T(1024)S(1)}, f32[2048]{0:T(1024)S(1)}, f32[2048]{0:T(1024)S(1)}, f32[2048]{0:T(1024)S(1)}, /*index=5*/f32[...) fusion(bf16[128,2048]{1,0:T(8,128)(2,1)} %get-tuple-element.1548, bf16[255,2048]{1,0:T(8,128)(2,1)S(1)} %get-tuple-element.1549, ...), kind=kLoop, calls=%fused_computation.45.clone.1 | loop fusion | flops 8634368 | bytes 4785184 | tf_op jit(solution)/shard_map/while/body/eval_jaxpr/reduce_sum | solution.py:75
  195.9 3.8 fusion.241
  199.7 4.0 %fusion.240 = (f32[2048]{0:T(1024)S(1)}, f32[2048]{0:T(1024)S(1)}, f32[2048]{0:T(1024)S(1)}, f32[2048]{0:T(1024)S(1)}, f32[2048]{0:T(1024)S(1)}, /*index=5*/f32[...) fusion(bf16[128,2048]{1,0:T(8,128)(2,1)} %get-tuple-element.1548, bf16[255,2048]{1,0:T(8,128)(2,1)S(1)} %get-tuple-element.1549, ...), kind=kLoop, calls=%fused_computation.45.clone.1 | loop fusion | flops 8634368 | bytes 4785184 | tf_op jit(solution)/shard_map/while/body/eval_jaxpr/reduce_sum | solution.py:75
  204.7 3.8 fusion.241
  208.5 4.0 %fusion.240 = (f32[2048]{0:T(1024)S(1)}, f32[2048]{0:T(1024)S(1)}, f32[2048]{0:T(1024)S(1)}, f32[2048]{0:T(1024)S(1)}, f32[2048]{0:T(1024)S(1)}, /*index=5*/f32[...) fusion(bf16[128,2048]{1,0:T(8,128)(2,1)} %get-tuple-element.1548, bf16[255,2048]{1,0:T(8,128)(2,1)S(1)} %get-tuple-element.1549, ...), kind=kLoop, calls=%fused_computation.45.clone.1 | loop fusion | flops 8634368 | bytes 4785184 | tf_op jit(solution)/shard_map/while/body/eval_jaxpr/reduce_sum | solution.py:75
  213.6 3.8 fusion.241
  217.4 4.0 %fusion.240 = (f32[2048]{0:T(1024)S(1)}, f32[2048]{0:T(1024)S(1)}, f32[2048]{0:T(1024)S(1)}, f32[2048]{0:T(1024)S(1)}, f32[2048]{0:T(1024)S(1)}, /*index=5*/f32[...) fusion(bf16[128,2048]{1,0:T(8,128)(2,1)} %get-tuple-element.1548, bf16[255,2048]{1,0:T(8,128)(2,1)S(1)} %get-tuple-element.1549, ...), kind=kLoop, calls=%fused_computation.45.clone.1 | loop fusion | flops 8634368 | bytes 4785184 | tf_op jit(solution)/shard_map/while/body/eval_jaxpr/reduce_sum | solution.py:75
  222.4 3.8 fusion.241
  226.3 4.0 %fusion.240 = (f32[2048]{0:T(1024)S(1)}, f32[2048]{0:T(1024)S(1)}, f32[2048]{0:T(1024)S(1)}, f32[2048]{0:T(1024)S(1)}, f32[2048]{0:T(1024)S(1)}, /*index=5*/f32[...) fusion(bf16[128,2048]{1,0:T(8,128)(2,1)} %get-tuple-element.1548, bf16[255,2048]{1,0:T(8,128)(2,1)S(1)} %get-tuple-element.1549, ...), kind=kLoop, calls=%fused_computation.45.clone.1 | loop fusion | flops 8634368 | bytes 4785184 | tf_op jit(solution)/shard_map/while/body/eval_jaxpr/reduce_sum | solution.py:75
  231.2 3.3 fusion.134
  235.9 69.8 %while.36 = (s32[]{:T(128)}, f32[128,2048]{1,0:T(8,128)}, s32[255]{0:T(256)S(1)}, f32[128,2048]{1,0:T(8,128)}, bf16[255,2048]{1,0:T(8,128)(2,1)S(1)}, /*index=5*...) while((s32[]{:T(128)}, f32[128,2048]{1,0:T(8,128)}, ...), condition=%wide.region_8.9_spmd.clone, body=%wide.region_7.8_spmd.clone.sunk | while | flops 17041508 | bytes 10893119 | solution.py:63
  238.0 5.8 %fusion.243 = f32[128,2048]{1,0:T(8,128)} fusion(f32[128,2048]{1,0:T(8,128)} %get-tuple-element.1388, bf16[255,2048]{1,0:T(8,128)(2,1)S(1)} %get-tuple-element.1445, s32[]{:T(128)S(6)} %select_n.2627, f32[2048]{0:T(1024)S(1)} %bitcast.458, s32[]{:T(128)S(6)} %select_n.2644, f32[2048]{0:T(1024)S(1)} %bitcast.459, s32[]{:T(128)S(6)} %select_n.2645, ...), kind=kLoop, calls=%fused_computation.128.clone.1 | loop fusion | flops 17039360 | bytes 10618945 | tf_op jit(solution)/shard_map/while/body/eval_jaxpr/add | solution.py:57
  245.9 6.8 %fusion.243 = f32[128,2048]{1,0:T(8,128)} fusion(f32[128,2048]{1,0:T(8,128)} %get-tuple-element.1388, bf16[255,2048]{1,0:T(8,128)(2,1)S(1)} %get-tuple-element.1445, s32[]{:T(128)S(6)} %select_n.2627, f32[2048]{0:T(1024)S(1)} %bitcast.458, s32[]{:T(128)S(6)} %select_n.2644, f32[2048]{0:T(1024)S(1)} %bitcast.459, s32[]{:T(128)S(6)} %select_n.2645, ...), kind=kLoop, calls=%fused_computation.128.clone.1 | loop fusion | flops 17039360 | bytes 10618945 | tf_op jit(solution)/shard_map/while/body/eval_jaxpr/add | solution.py:57
  254.6 6.8 %fusion.243 = f32[128,2048]{1,0:T(8,128)} fusion(f32[128,2048]{1,0:T(8,128)} %get-tuple-element.1388, bf16[255,2048]{1,0:T(8,128)(2,1)S(1)} %get-tuple-element.1445, s32[]{:T(128)S(6)} %select_n.2627, f32[2048]{0:T(1024)S(1)} %bitcast.458, s32[]{:T(128)S(6)} %select_n.2644, f32[2048]{0:T(1024)S(1)} %bitcast.459, s32[]{:T(128)S(6)} %select_n.2645, ...), kind=kLoop, calls=%fused_computation.128.clone.1 | loop fusion | flops 17039360 | bytes 10618945 | tf_op jit(solution)/shard_map/while/body/eval_jaxpr/add | solution.py:57
  263.6 6.8 %fusion.243 = f32[128,2048]{1,0:T(8,128)} fusion(f32[128,2048]{1,0:T(8,128)} %get-tuple-element.1388, bf16[255,2048]{1,0:T(8,128)(2,1)S(1)} %get-tuple-element.1445, s32[]{:T(128)S(6)} %select_n.2627, f32[2048]{0:T(1024)S(1)} %bitcast.458, s32[]{:T(128)S(6)} %select_n.2644, f32[2048]{0:T(1024)S(1)} %bitcast.459, s32[]{:T(128)S(6)} %select_n.2645, ...), kind=kLoop, calls=%fused_computation.128.clone.1 | loop fusion | flops 17039360 | bytes 10618945 | tf_op jit(solution)/shard_map/while/body/eval_jaxpr/add | solution.py:57
  272.3 6.8 %fusion.243 = f32[128,2048]{1,0:T(8,128)} fusion(f32[128,2048]{1,0:T(8,128)} %get-tuple-element.1388, bf16[255,2048]{1,0:T(8,128)(2,1)S(1)} %get-tuple-element.1445, s32[]{:T(128)S(6)} %select_n.2627, f32[2048]{0:T(1024)S(1)} %bitcast.458, s32[]{:T(128)S(6)} %select_n.2644, f32[2048]{0:T(1024)S(1)} %bitcast.459, s32[]{:T(128)S(6)} %select_n.2645, ...), kind=kLoop, calls=%fused_computation.128.clone.1 | loop fusion | flops 17039360 | bytes 10618945 | tf_op jit(solution)/shard_map/while/body/eval_jaxpr/add | solution.py:57
  281.3 6.8 %fusion.243 = f32[128,2048]{1,0:T(8,128)} fusion(f32[128,2048]{1,0:T(8,128)} %get-tuple-element.1388, bf16[255,2048]{1,0:T(8,128)(2,1)S(1)} %get-tuple-element.1445, s32[]{:T(128)S(6)} %select_n.2627, f32[2048]{0:T(1024)S(1)} %bitcast.458, s32[]{:T(128)S(6)} %select_n.2644, f32[2048]{0:T(1024)S(1)} %bitcast.459, s32[]{:T(128)S(6)} %select_n.2645, ...), kind=kLoop, calls=%fused_computation.128.clone.1 | loop fusion | flops 17039360 | bytes 10618945 | tf_op jit(solution)/shard_map/while/body/eval_jaxpr/add | solution.py:57
  290.0 6.8 %fusion.243 = f32[128,2048]{1,0:T(8,128)} fusion(f32[128,2048]{1,0:T(8,128)} %get-tuple-element.1388, bf16[255,2048]{1,0:T(8,128)(2,1)S(1)} %get-tuple-element.1445, s32[]{:T(128)S(6)} %select_n.2627, f32[2048]{0:T(1024)S(1)} %bitcast.458, s32[]{:T(128)S(6)} %select_n.2644, f32[2048]{0:T(1024)S(1)} %bitcast.459, s32[]{:T(128)S(6)} %select_n.2645, ...), kind=kLoop, calls=%fused_computation.128.clone.1 | loop fusion | flops 17039360 | bytes 10618945 | tf_op jit(solution)/shard_map/while/body/eval_jaxpr/add | solution.py:57
  299.0 6.8 %fusion.243 = f32[128,2048]{1,0:T(8,128)} fusion(f32[128,2048]{1,0:T(8,128)} %get-tuple-element.1388, bf16[255,2048]{1,0:T(8,128)(2,1)S(1)} %get-tuple-element.1445, s32[]{:T(128)S(6)} %select_n.2627, f32[2048]{0:T(1024)S(1)} %bitcast.458, s32[]{:T(128)S(6)} %select_n.2644, f32[2048]{0:T(1024)S(1)} %bitcast.459, s32[]{:T(128)S(6)} %select_n.2645, ...), kind=kLoop, calls=%fused_computation.128.clone.1 | loop fusion | flops 17039360 | bytes 10618945 | tf_op jit(solution)/shard_map/while/body/eval_jaxpr/add | solution.py:57
  305.8 3.1 fusion.155
  312.3 2.0 fusion.157
  315.2 2.7 fusion.178
  326.9 52.9 %all-reduce.4.cloned.1.call-done = (f32[3,7,2048]{2,1,0:T(8,128)}, f32[128,2048]{1,0:T(8,128)}) async-done(((f32[3,7,2048]{2,1,0:T(8,128)}, f32[128,2048]{1,0:T(8,128)}), (f32[3,7,2048]{2,1,0:T(8,128)}, f32[128,2048]{1,0:T(8,128)})) %all-reduce.4.cloned.1.call-update) | async-done | bytes 1220624 | tf_op jit(solution)/shard_map/psum | solution.py:138
  (254 shorter events, 68.8 us)
Async XLA Ops:
  7.2 372.7 %all-reduce.4.cloned.1.call-start = ((), (), s32[]{:S(2)}) async-start(), calls=%async_computation | async-start | bytes 2490368 | tf_op jit(solution)/shard_map/psum | solution.py:138
  8.1 25.3 %collective-permute-start = (bf16[3,6,2048]{2,1,0:T(8,128)(2,1)S(1)}, bf16[3,6,2048]{2,1,0:T(8,128)(2,1)S(1)}, u32[]{:S(2)}, u32[]{:S(2)}) collective-permute-start(bf16[3,6,2048]{2,1,0:T(8,128)(2,1)S(1)} %slice.171), channel_id=1, source_target_pairs={{0,1},{1,4},{4,5},{5,8},{8,9},{9,12},{12,13},{2,3},{3,6},{6,7},{7,... | collective-permute-start | bytes 221192 | tf_op jit(solution)/shard_map/ppermute | solution.py:14
  12.4 30.8 %copy-start.9 = (f32[1,1,2048]{2,1,0:T(1,128)}, f32[1,1,2048]{2,1,0:T(1,128)S(1)}, u32[]{:S(2)}) copy-start(f32[1,1,2048]{2,1,0:T(1,128)S(1)} %get-tuple-element.899) | copy-start | bytes 24580
  12.4 30.8 %copy-start.11 = (f32[1,1,2048]{2,1,0:T(1,128)}, f32[1,1,2048]{2,1,0:T(1,128)S(1)}, u32[]{:S(2)}) copy-start(f32[1,1,2048]{2,1,0:T(1,128)S(1)} %get-tuple-element.900) | copy-start | bytes 24580
  12.4 30.8 %copy-start.13 = (f32[1,1,2048]{2,1,0:T(1,128)}, f32[1,1,2048]{2,1,0:T(1,128)S(1)}, u32[]{:S(2)}) copy-start(f32[1,1,2048]{2,1,0:T(1,128)S(1)} %get-tuple-element.901) | copy-start | bytes 24580
  12.4 30.8 %copy-start.15 = (f32[1,1,2048]{2,1,0:T(1,128)}, f32[1,1,2048]{2,1,0:T(1,128)S(1)}, u32[]{:S(2)}) copy-start(f32[1,1,2048]{2,1,0:T(1,128)S(1)} %get-tuple-element.902) | copy-start | bytes 24580
  12.4 30.8 %copy-start.17 = (f32[1,1,2048]{2,1,0:T(1,128)}, f32[1,1,2048]{2,1,0:T(1,128)S(1)}, u32[]{:S(2)}) copy-start(f32[1,1,2048]{2,1,0:T(1,128)S(1)} %get-tuple-element.903) | copy-start | bytes 24580
  12.4 30.8 %copy-start.19 = (f32[1,1,2048]{2,1,0:T(1,128)}, f32[1,1,2048]{2,1,0:T(1,128)S(1)}, u32[]{:S(2)}) copy-start(f32[1,1,2048]{2,1,0:T(1,128)S(1)} %get-tuple-element.904) | copy-start | bytes 24580
  12.5 30.8 %copy-start.21 = (f32[1,1,2048]{2,1,0:T(1,128)}, f32[1,1,2048]{2,1,0:T(1,128)S(1)}, u32[]{:S(2)}) copy-start(f32[1,1,2048]{2,1,0:T(1,128)S(1)} %get-tuple-element.905) | copy-start | bytes 24580
  12.5 30.8 %copy-start.23 = (f32[1,1,2048]{2,1,0:T(1,128)}, f32[1,1,2048]{2,1,0:T(1,128)S(1)}, u32[]{:S(2)}) copy-start(f32[1,1,2048]{2,1,0:T(1,128)S(1)} %get-tuple-element.906) | copy-start | bytes 24580
  12.5 36.8 %copy-start.25 = (f32[1,1,2048]{2,1,0:T(1,128)}, f32[1,1,2048]{2,1,0:T(1,128)S(1)}, u32[]{:S(2)}) copy-start(f32[1,1,2048]{2,1,0:T(1,128)S(1)} %get-tuple-element.894) | copy-start | bytes 24580
  12.5 36.8 %copy-start.27 = (f32[1,1,2048]{2,1,0:T(1,128)}, f32[1,1,2048]{2,1,0:T(1,128)S(1)}, u32[]{:S(2)}) copy-start(f32[1,1,2048]{2,1,0:T(1,128)S(1)} %get-tuple-element.907) | copy-start | bytes 24580
  12.5 36.8 %copy-start.29 = (f32[1,1,2048]{2,1,0:T(1,128)}, f32[1,1,2048]{2,1,0:T(1,128)S(1)}, u32[]{:S(2)}) copy-start(f32[1,1,2048]{2,1,0:T(1,128)S(1)} %get-tuple-element.908) | copy-start | bytes 24580
  12.5 36.8 %copy-start.31 = (f32[1,1,2048]{2,1,0:T(1,128)}, f32[1,1,2048]{2,1,0:T(1,128)S(1)}, u32[]{:S(2)}) copy-start(f32[1,1,2048]{2,1,0:T(1,128)S(1)} %get-tuple-element.909) | copy-start | bytes 24580
  12.5 36.8 %copy-start.33 = (f32[1,1,2048]{2,1,0:T(1,128)}, f32[1,1,2048]{2,1,0:T(1,128)S(1)}, u32[]{:S(2)}) copy-start(f32[1,1,2048]{2,1,0:T(1,128)S(1)} %get-tuple-element.910) | copy-start | bytes 24580
  12.5 36.8 %copy-start.35 = (f32[1,1,2048]{2,1,0:T(1,128)}, f32[1,1,2048]{2,1,0:T(1,128)S(1)}, u32[]{:S(2)}) copy-start(f32[1,1,2048]{2,1,0:T(1,128)S(1)} %get-tuple-element.911) | copy-start | bytes 24580
  12.5 36.8 %copy-start.37 = (f32[1,1,2048]{2,1,0:T(1,128)}, f32[1,1,2048]{2,1,0:T(1,128)S(1)}, u32[]{:S(2)}) copy-start(f32[1,1,2048]{2,1,0:T(1,128)S(1)} %get-tuple-element.912) | copy-start | bytes 24580
  13.5 29.7 %copy-start.39 = (f32[1,1,2048]{2,1,0:T(1,128)}, f32[1,1,2048]{2,1,0:T(1,128)S(1)}, u32[]{:S(2)}) copy-start(f32[1,1,2048]{2,1,0:T(1,128)S(1)} %get-tuple-element.913) | copy-start | bytes 24580
  13.5 29.7 %copy-start.41 = (f32[1,1,2048]{2,1,0:T(1,128)}, f32[1,1,2048]{2,1,0:T(1,128)S(1)}, u32[]{:S(2)}) copy-start(f32[1,1,2048]{2,1,0:T(1,128)S(1)} %get-tuple-element.914) | copy-start | bytes 24580
  15.1 31.4 %copy-start.6 = (s32[255]{0:T(256)}, s32[255]{0:T(256)S(1)}, u32[]{:S(2)}) copy-start(s32[255]{0:T(256)S(1)} %fusion.225) | copy-start | bytes 3064
  15.8 33.5 %copy-start.46 = (pred[128]{0:T(512)(128)(4,1)}, pred[128]{0:T(512)(128)(4,1)S(1)}, u32[]{:S(2)}) copy-start(pred[128]{0:T(512)(128)(4,1)S(1)} %get-tuple-element.922) | copy-start | bytes 388
  15.8 33.5 %copy-start.48 = (pred[128]{0:T(512)(128)(4,1)}, pred[128]{0:T(512)(128)(4,1)S(1)}, u32[]{:S(2)}) copy-start(pred[128]{0:T(512)(128)(4,1)S(1)} %get-tuple-element.917) | copy-start | bytes 388
  15.8 33.6 %copy-start.50 = (pred[128]{0:T(512)(128)(4,1)}, pred[128]{0:T(512)(128)(4,1)S(1)}, u32[]{:S(2)}) copy-start(pred[128]{0:T(512)(128)(4,1)S(1)} %get-tuple-element.918) | copy-start | bytes 388
  15.8 33.6 %copy-start.52 = (pred[128]{0:T(512)(128)(4,1)}, pred[128]{0:T(512)(128)(4,1)S(1)}, u32[]{:S(2)}) copy-start(pred[128]{0:T(512)(128)(4,1)S(1)} %get-tuple-element.919) | copy-start | bytes 388
  15.8 33.6 %copy-start.54 = (pred[128]{0:T(512)(128)(4,1)}, pred[128]{0:T(512)(128)(4,1)S(1)}, u32[]{:S(2)}) copy-start(pred[128]{0:T(512)(128)(4,1)S(1)} %get-tuple-element.920) | copy-start | bytes 388
  15.8 33.6 %copy-start.56 = (pred[128]{0:T(512)(128)(4,1)}, pred[128]{0:T(512)(128)(4,1)S(1)}, u32[]{:S(2)}) copy-start(pred[128]{0:T(512)(128)(4,1)S(1)} %get-tuple-element.921) | copy-start | bytes 388
  33.4 12.9 %copy-start.66 = (s32[8]{0:T(128)S(1)}, s32[8]{0:T(128)}, u32[]{:S(2)}) copy-start(s32[8]{0:T(128)} %param.19) | copy-start | bytes 100
  43.3 4.9 %copy-start.68 = (u32[32]{0:T(128)S(1)}, u32[32]{0:T(128)}, u32[]{:S(2)}) copy-start(u32[32]{0:T(128)} %constant.1242) | copy-start | bytes 388
  43.3 6.1 %copy-start = (bf16[3,128,2048]{2,1,0:T(8,128)(2,1)S(1)}, bf16[3,128,2048]{2,1,0:T(8,128)(2,1)}, u32[]{:S(2)}) copy-start(bf16[3,128,2048]{2,1,0:T(8,128)(2,1)} %param.13) | copy-start | bytes 4718596
  44.2 7.0 %collective-permute-start.1 = (bf16[127,2048]{1,0:T(8,128)(2,1)S(1)}, bf16[127,2048]{1,0:T(8,128)(2,1)}, u32[]{:S(2)}, u32[]{:S(2)}) collective-permute-start(bf16[127,2048]{1,0:T(8,128)(2,1)S(1)} %slice.175), channel_id=1, source_target_pairs={{0,1},{1,4},{4,5},{5,8},{8,9},{9,12},{12,13},{2,3},{3,6},{6,7},{7,... | collective-permute-start | bytes 1560584 | tf_op jit(solution)/shard_map/ppermute | solution.py:14
  52.6 68.4 %copy-start.8 = (f32[2048]{0:T(1024)S(1)}, f32[2048]{0:T(1024)}, u32[]{:S(2)}) copy-start(f32[2048]{0:T(1024)} %param.17) | copy-start | bytes 24580
  52.6 70.5 %copy-start.69 = (s32[128]{0:T(128)S(1)}, s32[128]{0:T(128)}, u32[]{:S(2)}) copy-start(s32[128]{0:T(128)} %slice.170) | copy-start | bytes 1540
  121.0 34.1 %copy-start.65 = (s32[8]{0:T(128)S(1)}, s32[8]{0:T(128)}, u32[]{:S(2)}) copy-start(s32[8]{0:T(128)} %param.18) | copy-start | bytes 100
  121.0 34.2 %copy-start.67 = (s32[8]{0:T(128)S(1)}, s32[8]{0:T(128)}, u32[]{:S(2)}) copy-start(s32[8]{0:T(128)} %param.19) | copy-start | bytes 100
  155.5 4.8 %copy-start.64 = (f32[128]{0:T(128)}, f32[128]{0:T(128)S(1)}, u32[]{:S(2)}) copy-start(f32[128]{0:T(128)S(1)} %convolution_bitcast_fusion.1) | copy-start | bytes 1540
  157.7 76.9 %collective-permute-start.2 = (bf16[127,2048]{1,0:T(8,128)(2,1)}, bf16[127,2048]{1,0:T(8,128)(2,1)}, u32[]{:S(2)}, u32[]{:S(2)}) collective-permute-start(bf16[127,2048]{1,0:T(8,128)(2,1)} %bitcast.322), channel_id=1, source_target_pairs={{1,0},{4,1},{5,4},{8,5},{9,8},{12,9},{13,12},{3,2},{6,3},{7,6},{10... | collective-permute-start | bytes 1560584 | tf_op jit(solution)/shard_map/ppermute | solution.py:14
  160.3 71.0 %copy-start.3 = (bf16[128,2048]{1,0:T(8,128)(2,1)S(1)}, bf16[128,2048]{1,0:T(8,128)(2,1)}, u32[]{:S(2)}) copy-start(bf16[128,2048]{1,0:T(8,128)(2,1)} %param.16) | copy-start | bytes 1572868
  235.9 69.9 %copy-start.55 = (pred[128]{0:T(512)(128)(4,1)S(1)}, pred[128]{0:T(512)(128)(4,1)}, u32[]{:S(2)}) copy-start(pred[128]{0:T(512)(128)(4,1)} %copy-done.54) | copy-start | bytes 388
  235.9 69.9 %copy-start.57 = (pred[128]{0:T(512)(128)(4,1)S(1)}, pred[128]{0:T(512)(128)(4,1)}, u32[]{:S(2)}) copy-start(pred[128]{0:T(512)(128)(4,1)} %copy-done.56) | copy-start | bytes 388
  305.7 3.2 copy-start.1
  305.7 3.2 copy-start.4
  305.7 3.2 copy-start.5
  305.8 3.1 copy-start.47
  310.0 2.3 copy-start.51
  310.0 2.3 copy-start.53
  310.7 8.9 %collective-permute-start.3 = (bf16[3,6,2048]{2,1,0:T(8,128)(2,1)}, bf16[3,6,2048]{2,1,0:T(8,128)(2,1)S(1)}, u32[]{:S(2)}, u32[]{:S(2)}) collective-permute-start(bf16[3,6,2048]{2,1,0:T(8,128)(2,1)} %pad_maximum_fusion.6), channel_id=1, source_target_pairs={{1,0},{4,1},{5,4},{8,5},{9,8},{12,9},{13,12},{3,2},{6,3},{7,6},{10... | collective-permute-start | bytes 221192 | tf_op jit(solution)/shard_map/ppermute | solution.py:14
  314.3 3.6 copy-start.44
  314.3 3.6 copy-start.45
  (28 other events, 34.9 us)
Sparse Core Ops, SparseCore 0:
  319.5 60.2 all-reduce.3
